TPU v7x, 128 devices: a whole 4x4x4 slice. The times are simulated.
128 devices in a mesh: space: 32 (over y, x, core), probe: 4 (over z).
Axes of the slice: x: 4, y: 4, z: 4, core: 2. Of those that a mesh axis runs over, the one named last changes fastest.
Arguments:
- points: float32 [1024, 3, 512], P('space')
- probes: float32 [1024, 32, 512], P('space', 'probe'), may hold values from -6 to 6
- counts: int32 [1024], P('space'), may hold values from 128 to 512, as said below
- near_list: int32 [1024, 8], P('space'), may hold values from 0 to 1023, as said below
- far_list: int32 [1024, 32], P('space'), may hold values from 0 to 1023, as said below
- coarse_list: int32 [56, 16], replicated, may hold values from 0 to 31, as said below
- leaf_proxy: float32 [1024, 3, 64], P('space')
- box_proxy: float32 [56, 3, 64], replicated
Outputs:
- result: float32 [1024, 32, 512], P('space', 'probe')
Inputs may be any that keep to these rules, and one draw needn't show every extreme that they name: `counts`: the first leaf of every block of 32 is full. `near_list`: entry 0 of row i is i; every entry lies within 32 of its row's index. `far_list`: every entry lies within 32 of its row's index. `coarse_list`: rows 0 to 31 belong to device boxes, the next 16 to pair boxes, the last 8 to quad boxes; each entry is a box index within its row's level and never the row's own box.
All inputs are finite; a program needn't handle non-finite values.
Results may differ from a plain program's by a relative error of at most 0.00018.
Values sent between devices are 32-bit elements; how exact they have to be, the bound alone decides.
No kernel may reach another device: no remote copies, remote signals or barrier semaphores. Data moves between devices by JAX's collectives and lax.ppermute only.
A program may use at most 64 MiB of HBM per device.

v0:
```python
import functools

import jax
import jax.numpy as jnp
from jax import lax
from jax.experimental import pallas as pl
from jax.experimental.pallas import tpu as pltpu
from jax.sharding import PartitionSpec as P

F32 = jnp.float32
BF16 = jnp.bfloat16
LOG2E = 1.4426950408889634
LN2 = 0.6931471805599453
SCALE = LOG2E * 1.7320508075688772 / 2.0
SLOPE = 0.5 / (LOG2E * LOG2E)
TINY = 1e-30
FEATURES = 48
UNITS = 8
CN = (((0,), (0,)), ((), ()))
NT = (((1,), (1,)), ((), ()))
NN = (((1,), (0,)), ((), ()))


def dot(left, right, dims):
    return lax.dot_general(left, right, dims, preferred_element_type=F32)


def split(value):
    high = value.astype(BF16)
    return high, (value - high.astype(F32)).astype(BF16)


def stacked(value):
    high = value.astype(BF16).astype(F32)
    return jnp.concatenate([high, value - high], axis=0).astype(BF16)


def exact_dot(left, right, dims):
    rows = left.shape[0]
    high, low = split(right)
    both = stacked(left)
    total = dot(both, high, dims) + dot(both, low, dims)
    return total[:rows] + total[rows:]


def slope_of(u):
    u = jnp.maximum(u, TINY)
    return u * jnp.exp2(-(u * lax.rsqrt(u)))


def value_of(u):
    u = jnp.maximum(u, TINY)
    w = u * lax.rsqrt(u)
    return (1.0 + LN2 * w) * jnp.exp2(-w)


def pieces(value):
    high = value.astype(BF16).astype(F32)
    rest = value - high
    middle = rest.astype(BF16).astype(F32)
    return high, middle, rest - middle


def features(rows, center, source, target):
    row = lax.broadcasted_iota(jnp.int32, rows.shape, 0)
    scaled = jnp.where(row < 3, (rows - center) * SCALE, 0.0)
    norm = jnp.sum(scaled * scaled, axis=0, keepdims=True)
    out = []
    if source:
        h, m, l = pieces(jnp.where(row == 3, norm, jnp.where(row == 4, 1.0, scaled)))
        out.append(jnp.concatenate([h, h, m, h, l, m], axis=0))
    if target:
        h, m, l = pieces(jnp.where(row == 3, 1.0, jnp.where(row == 4, norm, -2.0 * scaled)))
        out.append(jnp.concatenate([h, m, h, l, h, m], axis=0))
    return out


def twice(value):
    return jnp.concatenate([value, value], axis=1)


def left_half(shape):
    return lax.broadcasted_iota(jnp.int32, shape, 1) < 64


def lanes_of(page, i, start):
    return jnp.concatenate([page[i, 16 * b + start : 16 * b + start + 8, :] for b in range(4)], axis=1)


def partner_of(page, i):
    return jnp.concatenate([page[i, 80 + 8 * b : 88 + 8 * b, :] for b in range(4)], axis=1)


def center_of(page):
    return page[0, 8:16, 0:1]


def store_source(slot, page, i, partner, center, fs, ms):
    rows = lanes_of(page, i, 8)
    (source,) = features(rows, center, True, False)
    source = source.astype(BF16)
    lane = lax.broadcasted_iota(jnp.int32, partner.shape, 1).astype(F32)
    other = jnp.where(lane < rows[3:4], partner, 0.0)
    moments = stacked(jnp.concatenate([lanes_of(page, i, 0), other], axis=0))
    for b in range(4):
        fs[slot * 4 + b] = source[:, b * 128 : (b + 1) * 128]
        ms[slot * 4 + b] = moments[:, b * 128 : (b + 1) * 128]


def store_target(slot, page, i, center, ft):
    (target,) = features(lanes_of(page, i, 8), center, False, True)
    target = target.astype(BF16)
    for b in range(2):
        ft[slot * 2 + b] = target[:, b * 256 : (b + 1) * 256]


def build_items(place, target_count, targets, empty, blocks, items):
    def per_leaf(i, n):
        nb = jnp.int32(0)
        for e in range(8):
            ok, slot, count = place(i, e)
            for b in range(4):
                blocks[nb + b] = slot * 4 + b
            nb = nb + jnp.where(ok, (count + 127) >> 7, 0)
        blocks[nb] = empty
        pairs = (nb + 1) >> 1

        def put(q, carry):
            code = (blocks[2 * q] << 9) | blocks[2 * q + 1]
            items[n + q] = code | ((2 * i) << 18)
            items[n + pairs + q] = code | ((2 * i + 1) << 18)
            return carry

        lax.fori_loop(0, pairs, put, 0)
        return n + jnp.where(target_count(i) > 256, 2 * pairs, pairs)

    n = lax.fori_loop(0, targets, per_leaf, jnp.int32(0))
    for t in range(2 * UNITS):
        items[n + t] = (empty << 9) | empty
    return n


def run_items(items, n, fs, ft, ms, acc, slots):
    def distances(code, u):
        left = jnp.concatenate([fs[(code >> 9) & 511], fs[code & 511]], axis=1)
        u[...] = dot(left, ft[code >> 18], CN)

    def contract(code, u):
        high, low = split(slope_of(u[...]))
        m = jnp.concatenate([ms[(code >> 9) & 511], ms[code & 511]], axis=1)
        acc[code >> 18] += dot(m, high, NN) + dot(m, low, NN)

    for s in range(UNITS):
        distances(items[s], slots[s])

    def body(t, carry):
        for s in range(UNITS):
            contract(items[UNITS * t + s], slots[s])
            distances(items[UNITS * (t + 1) + s], slots[s])
        return carry

    lax.fori_loop(0, (n + UNITS - 1) // UNITS, body, 0)


def rows_of(planes, i, extra):
    rows = [planes[d, pl.ds(i, 1), :] for d in range(3)]
    width = rows[0].shape[1]
    return jnp.concatenate(
        rows + [jnp.full((1, width), extra, F32), jnp.zeros((4, width), F32)], axis=0
    )


def moments_kernel(counts, me, probes, points, leafp, boxp, page, dev, fp, *, leaves, factor):
    c = rows_of(points, 0, 0.0)[:, 0:1]
    (own_target,) = features(rows_of(boxp, me[0], 0.0), c, False, True)
    own_target = own_target.astype(BF16)
    lane = lax.broadcasted_iota(jnp.int32, probes.shape[1:], 1)

    def prep(i):
        count = counts[i]
        masked = jnp.where(lane < count, probes[i], 0.0)
        rows = rows_of(points, i, count.astype(F32))
        for b in range(4):
            page[i, 16 * b : 16 * b + 8, :] = masked[:, b * 128 : (b + 1) * 128]
            page[i, 16 * b + 8 : 16 * b + 16, :] = rows[:, b * 128 : (b + 1) * 128]
        proxies = twice(rows_of(leafp, i, 0.0))
        page[i, 72:80, :] = proxies
        (target,) = features(rows, c, False, True)
        (fp[i],) = features(proxies, c, True, False)
        return masked, target.astype(BF16)

    def body(t, carry):
        for s in range(4):
            i = t * 8 + 2 * s
            (left, left_points), (right, right_points) = prep(i), prep(i + 1)
            both = jnp.concatenate([left_points, right_points], axis=0)
            basis = value_of(dot(both, shared(fp[i], fp[i + 1]), CN))
            pair = exact_dot(jnp.concatenate([left, right], axis=0), basis, NN) * factor
            page[i, 64:72, :] = twice(pair[0:8, 0:64])
            page[i + 1, 64:72, :] = twice(pair[8:16, 64:128])
        return carry

    lax.fori_loop(0, leaves // 8, body, 0)
    half = left_half((FEATURES, 128))
    half8 = left_half((8, 128))
    total = jnp.zeros((8, 64), F32)
    for g in range(leaves // 8):
        sources, moments = [], []
        for q in range(4):
            i = 8 * g + 2 * q
            sources.append(jnp.where(half, fp[i], fp[i + 1]).astype(BF16))
            moments.append(jnp.where(half8, page[i, 64:72, :], page[i + 1, 64:72, :]))
        panel = value_of(dot(jnp.concatenate(sources, axis=1), own_target, CN))
        total = total + exact_dot(jnp.concatenate(moments, axis=1), panel, NN)
    dev[...] = twice(total * (1.0 / 64))


def assign(count_of, leaves, order):
    def tally(i, n):
        return n + (count_of(i) > 256).astype(jnp.int32)

    odd = lax.fori_loop(0, leaves, tally, jnp.int32(0)) & 1

    def deal(i, carry):
        large, taken = carry
        wide_leaf = (count_of(i) > 256).astype(jnp.int32)
        rank = jnp.where(wide_leaf == 1, large, i - large + odd)
        side = rank & 1
        place = jnp.where(side == 1, taken, i - taken)
        order[side * (leaves // 2) + place] = i
        return large + wide_leaf, taken + side

    lax.fori_loop(0, leaves, deal, (jnp.int32(0), jnp.int32(0)))


def clear_empty(empty, fs, ms):
    fs[empty] = jnp.zeros(fs.shape[1:], BF16)
    ms[empty] = jnp.zeros(ms.shape[1:], BF16)


def own_kernel(
    near, counts, me, page, partner, acc,
    fs, ms, ft, blocks, items, order, *slots, leaves, targets,
):
    c = center_of(page)
    assign(lambda i: counts[i], leaves, order)
    first = me[1] * targets

    def prep(t, carry):
        for s in range(8):
            i = 8 * t + s
            store_source(i, page, i, partner[i], c, fs, ms)
        for s in range(4):
            i = 4 * t + s
            store_target(i, page, order[first + i], c, ft)
        return carry

    lax.fori_loop(0, leaves // 8, prep, 0)
    clear_empty(leaves * 4, fs, ms)
    acc[...] = jnp.zeros_like(acc)

    def place(i, e):
        j = near[e, order[first + i]] - me[0] * leaves
        ok = (j >= 0) & (j < leaves)
        slot = jnp.where(ok, j, 0)
        return ok, slot, counts[slot]

    n = build_items(place, lambda i: counts[order[first + i]], targets, leaves * 4, blocks, items)
    run_items(items, n, fs, ft, ms, acc, slots)


def halo_kernel(
    near, counts, me, own, low, high, acc0,
    mine, theirs,
    acc, fs, ms, ft, blocks, items, order, *slots, leaves, targets, factor,
):
    c = center_of(own)
    assign(lambda i: counts[leaves + i], leaves, order)
    first = me[1] * targets

    def prep(t, carry):
        for s in range(4):
            i = 4 * t + s
            store_source(i, low, i, partner_of(low, i), c, fs, ms)
            store_source(leaves + i, high, i, partner_of(high, i), c, fs, ms)
        for s in range(2):
            i = 2 * t + s
            store_target(i, own, order[first + i], c, ft)
        return carry

    lax.fori_loop(0, leaves // 4, prep, 0)
    empty = 2 * leaves * 4
    clear_empty(empty, fs, ms)
    acc[...] = acc0[...]

    def place(i, e):
        j = near[e, order[first + i]] - (me[0] - 1) * leaves
        ok = (j < leaves) | (j >= 2 * leaves)
        slot = jnp.where(ok, jnp.where(j < leaves, j, j - leaves), 0)
        return ok, slot, counts[jnp.where(ok, j, 0)]

    n = build_items(place, lambda i: counts[leaves + order[first + i]], targets, empty, blocks, items)
    run_items(items, n, fs, ft, ms, acc, slots)
    scale = SLOPE * factor

    def finish(t, carry):
        for s in range(4):
            i = 4 * t + s
            for b in range(2):
                total = acc[2 * i + b]
                total = (total[0:16] + total[16:32]) * scale
                mine[i, :, b * 256 : (b + 1) * 256] = total[0:8]
                theirs[i, :, b * 256 : (b + 1) * 256] = total[8:16]
        return carry

    lax.fori_loop(0, targets // 4, finish, 0)


def far_sum(lists, count, source_of, moment_of, target):
    half = left_half((FEATURES, 128))
    half8 = left_half((8, 128))
    total = jnp.zeros((8, 64), F32)
    for chunk in range(count // 8):
        sources, moments = [], []
        for q in range(4):
            a, b = lists(chunk * 8 + 2 * q), lists(chunk * 8 + 2 * q + 1)
            sources.append(jnp.where(half, source_of(a), source_of(b)).astype(BF16))
            moments.append(jnp.where(half8, moment_of(a), moment_of(b)))
        sources = jnp.concatenate(sources, axis=1)
        moments = jnp.concatenate(moments, axis=1)
        total = total + exact_dot(moments, slope_of(dot(sources, target, CN)), NN)
    return total * (SLOPE / 64)


def shared(left, right):
    half = left_half(left.shape)
    pair = [jnp.where(half, left, 0.0), jnp.where(half, 0.0, right)]
    return jnp.concatenate(pair, axis=0).astype(BF16)


def own_halves(rows):
    return jnp.where(left_half((8, 128)), rows[0:8], rows[8:16])


def far_pair(lists, source_of, moment_of, target):
    half = left_half((FEATURES, 128))
    half8 = left_half((8, 128))
    total = jnp.zeros((16, 128), F32)
    for chunk in range(4):
        sources, moments = [], []
        for of in lists:
            row, moment = [], []
            for q in range(4):
                a, b = of(chunk * 8 + 2 * q), of(chunk * 8 + 2 * q + 1)
                row.append(jnp.where(half, source_of(a), source_of(b)).astype(BF16))
                moment.append(jnp.where(half8, moment_of(a), moment_of(b)))
            sources.append(jnp.concatenate(row, axis=1))
            moments.append(jnp.concatenate(moment, axis=1))
        panel = slope_of(dot(jnp.concatenate(sources, axis=0), target, CN))
        total = total + exact_dot(jnp.concatenate(moments, axis=0), panel, NN)
    return own_halves(total) * (SLOPE / 64)


def upper_levels(coarse, me, box8, roots, c, fbs, fbt, pm, qm):
    def prep(t, carry):
        for s in range(8):
            b = 8 * t + s
            fbs[b], fbt[b] = features(twice(rows_of(box8, b, 0.0)), c, True, True)
        return carry

    lax.fori_loop(0, 7, prep, 0)
    half = left_half((FEATURES, 128))
    half8 = left_half((8, 128))

    def merge(child, parent, moments, out, count):
        def body(t, carry):
            for s in range(8):
                m = t * 8 + s
                source = jnp.where(half, fbs[child + 2 * m], fbs[child + 2 * m + 1]).astype(BF16)
                target = fbt[parent + m].astype(BF16)[:, :64]
                panel = value_of(dot(source, target, CN))
                pair = jnp.where(half8, moments[2 * m], moments[2 * m + 1])
                out[m] = twice(exact_dot(pair, panel, NN) * (1.0 / 64))
            return carry

        lax.fori_loop(0, count // 8, body, 0)

    merge(0, 32, roots, pm, 16)
    merge(32, 48, pm, qm, 8)
    n = me
    m = n >> 1
    t = n >> 2

    def far(base, row, moments):
        target = fbt[row].astype(BF16)[:, :64]
        return far_sum(
            lambda e: coarse[e, row], 16, lambda b: fbs[base + b], lambda b: moments[b], target
        )

    def down(local, source, target):
        panel = value_of(dot(fbs[source].astype(BF16)[:, :64], fbt[target].astype(BF16)[:, :64], CN))
        return exact_dot(local, panel, NN) * (1.0 / 64)

    quad = far(48, 48 + t, qm)
    pair = down(quad, 48 + t, 32 + m) + far(32, 32 + m, pm)
    return down(pair, 32 + m, n) + far(0, n, roots)


def far_kernel(
    far, coarse, me, own, low, high, box8, roots,
    out,
    fps, fpt, mps, fbs, fbt, pm, qm, local,
    *, leaves, factor,
):
    c = center_of(own)

    def prep_far(t, carry):
        for s in range(4):
            i = t * 4 + s
            for k, (page, at) in enumerate(((low, 0), (own, 64), (high, 0))):
                (fps[k * leaves + i],) = features(page[i, at + 8 : at + 16], c, True, False)
                mps[k * leaves + i] = page[i, at : at + 8]
            (fpt[i],) = features(own[i, 72:80], c, False, True)
        return carry

    lax.fori_loop(0, leaves // 4, prep_far, 0)
    dev = me[0]
    base = (dev - 1) * leaves

    def gather(t, carry):
        for s in range(2):
            k = t * 2 + s
            local[k] = far_pair(
                [lambda e: far[2 * k, e] - base, lambda e: far[2 * k + 1, e] - base],
                lambda b: fps[b], lambda b: mps[b], shared(fpt[2 * k], fpt[2 * k + 1]),
            )
        return carry

    lax.fori_loop(0, leaves // 4, gather, 0)
    local_dev = upper_levels(coarse, dev, box8, roots, c, fbs, fbt, pm, qm)
    own_source = fbs[dev].astype(BF16)[:, :64]
    half = left_half((FEATURES, 128))

    def down(t, carry):
        for s in range(8):
            k = t * 8 + s
            target = jnp.where(half, fpt[2 * k], fpt[2 * k + 1]).astype(BF16)
            panel = value_of(dot(own_source, target, CN))
            local[k] += exact_dot(local_dev, panel, NN) * (1.0 / 64)
        return carry

    lax.fori_loop(0, leaves // 16, down, 0)

    def finish(t, carry):
        for s in range(8):
            i = t * 8 + s
            source = fps[leaves + i].astype(BF16)[:, :64]
            (points,) = features(lanes_of(own, i, 8), c, False, True)
            basis = value_of(dot(source, points.astype(BF16), CN))
            part = local[t * 4 + s // 2][:, (s % 2) * 64 : (s % 2) * 64 + 64]
            out[i] = exact_dot(part, basis, NN) * factor
        return carry

    lax.fori_loop(0, leaves // 8, finish, 0)


def sum_kernel(counts, me, far, mine, back, out, order, *, leaves):
    assign(lambda i: counts[i], leaves, order)
    half = leaves // 2
    lane = lax.broadcasted_iota(jnp.int32, far.shape[1:], 1)

    def body(t, carry):
        for s in range(4):
            k = 4 * t + s
            for side, part in ((me[1], mine), (1 - me[1], back)):
                i = order[side * half + k]
                out[i] = jnp.where(lane < counts[i], far[i] + part[k], 0.0)
        return carry

    lax.fori_loop(0, half // 4, body, 0)


def cost(microseconds):
    flops = int(microseconds * 1.1e9)
    return pl.CostEstimate(flops=flops, transcendentals=0, bytes_accessed=1 << 20)


def local(points, probes, counts, near_list, far_list, coarse_list, leaf_proxy, box_proxy):
    leaves = points.shape[0]
    size = points.shape[2]
    nodes = lax.axis_size("space")
    device = lax.axis_index("space")
    factor = size ** (-0.5)
    half = lax.axis_index("probe") & 1
    me = jnp.stack([device, half]).astype(jnp.int32)
    points = jnp.transpose(points, (1, 0, 2))
    leafp = jnp.transpose(leaf_proxy, (1, 0, 2))
    boxp = jnp.transpose(box_proxy, (1, 0, 2))
    near = near_list.T
    forward = [(i, i + 1) for i in range(nodes - 1)]
    backward = [(i + 1, i) for i in range(nodes - 1)]
    pairs = [(i, i ^ 1) for i in range(lax.axis_size("probe"))]
    partner = lax.ppermute(probes, "probe", pairs)
    params = pltpu.CompilerParams(vmem_limit_bytes=56 << 20)
    vm = pltpu.VMEM
    vmem = pl.BlockSpec(memory_space=vm)
    smem = pl.BlockSpec(memory_space=pltpu.SMEM)
    shape = jax.ShapeDtypeStruct
    page, dev = pl.pallas_call(
        functools.partial(moments_kernel, leaves=leaves, factor=factor),
        out_shape=(shape((leaves, 80, 128), F32), shape((8, 128), F32)),
        in_specs=[smem] * 2 + [vmem] * 4,
        out_specs=(vmem, vmem),
        scratch_shapes=[vm((leaves, FEATURES, 128), F32)],
        compiler_params=params,
        cost_estimate=cost(8),
        name="moments",
    )(counts, me, probes, points, leafp, boxp)
    roots = lax.all_to_all(
        jnp.broadcast_to(dev[None], (nodes, 8, 128)), "space", split_axis=0, concat_axis=0, tiled=True
    )
    tiles = jnp.transpose(partner.reshape(leaves, 8, size // 128, 128), (0, 2, 1, 3))
    both = jnp.concatenate([page, tiles.reshape(leaves, size // 16, 128)], axis=1)
    low = lax.ppermute(both, "space", forward)
    high = lax.ppermute(both, "space", backward)
    targets = leaves // 2

    def work(blocks):
        return (
            [
                vm((blocks, FEATURES, 128), BF16),
                vm((blocks, 32, 128), BF16),
                vm((targets * 2, FEATURES, 256), BF16),
                pltpu.SMEM((48,), jnp.int32),
                pltpu.SMEM((targets * 32 + 64,), jnp.int32),
                pltpu.SMEM((leaves,), jnp.int32),
            ]
            + [vm((256, 256), F32)] * UNITS
        )

    page, roots = lax.optimization_barrier((page, roots))
    acc0 = pl.pallas_call(
        functools.partial(own_kernel, leaves=leaves, targets=targets),
        out_shape=shape((targets * 2, 32, 256), F32),
        in_specs=[smem] * 3 + [vmem] * 2,
        out_specs=vmem,
        scratch_shapes=work(leaves * 4 + 1),
        compiler_params=params,
        cost_estimate=cost(28),
        name="near_own",
    )(near, counts, me, page, partner)
    counts3 = jnp.concatenate(
        [low[:, 11, 0].astype(jnp.int32), counts, high[:, 11, 0].astype(jnp.int32)]
    )
    mine, theirs = pl.pallas_call(
        functools.partial(halo_kernel, leaves=leaves, targets=targets, factor=factor),
        out_shape=(shape((targets, 8, size), F32),) * 2,
        in_specs=[smem] * 3 + [vmem] * 4,
        out_specs=(vmem, vmem),
        scratch_shapes=[vm((targets * 2, 32, 256), F32)] + work(2 * leaves * 4 + 1),
        compiler_params=params,
        cost_estimate=cost(30),
        name="near_halo",
    )(near, counts3, me, page, low, high, acc0)
    back = lax.ppermute(theirs, "probe", pairs)
    whole = lambda dims: pl.BlockSpec(dims, lambda i: (0,) * len(dims))
    tail = pl.BlockSpec((leaves, 16, 128), lambda i: (0, 4, 0))
    far = pl.pallas_call(
        functools.partial(far_kernel, leaves=leaves, factor=factor),
        out_shape=shape(probes.shape, F32),
        grid=(1,),
        in_specs=[smem] * 3 + [whole(page.shape), tail, tail, whole(boxp.shape), whole(roots.shape)],
        out_specs=whole(probes.shape),
        scratch_shapes=[
            vm((3 * leaves, FEATURES, 128), F32),
            vm((leaves, FEATURES, 128), F32),
            vm((3 * leaves, 8, 128), F32),
            vm((56, FEATURES, 128), F32),
            vm((56, FEATURES, 128), F32),
            vm((nodes // 2, 8, 128), F32),
            vm((nodes // 4, 8, 128), F32),
            vm((leaves // 2, 8, 128), F32),
        ],
        compiler_params=params,
        cost_estimate=cost(30),
        name="far",
    )(far_list, coarse_list.T, me, page, low, high, boxp, roots)
    return pl.pallas_call(
        functools.partial(sum_kernel, leaves=leaves),
        out_shape=shape(probes.shape, F32),
        in_specs=[smem] * 2 + [vmem] * 3,
        out_specs=vmem,
        scratch_shapes=[pltpu.SMEM((leaves,), jnp.int32)],
        compiler_params=params,
        name="sum",
    )(counts, me, far, mine, back)


def solution(mesh):
    return jax.shard_map(
        local,
        mesh=mesh,
        in_specs=(
            P("space", None, None),
            P("space", "probe", None),
            P("space"),
            P("space", None),
            P("space", None),
            P(),
            P("space", None, None),
            P(),
        ),
        out_specs=P("space", "probe", None),
        check_vma=False,
    )
```

profile of v0, /device:TPU:8, one launch (start us, length us, event | category | flops | bytes accessed | tf_op | source)
XLA Modules:
  0.0 121.0 jit_solution(5616372599359330715)
XLA Ops:
  0.0 1.9 %collective-permute-start = (f32[32,8,512]{2,1,0:T(8,128)}, f32[32,8,512]{2,1,0:T(8,128)S(1)}, u32[]{:S(2)}, u32[]{:S(2)}) collective-permute-start(f32[32,8,512]{2,1,0:T(8,128)} %probes.1), channel_id=1, source_target_pairs={{0,1},{1,0},{2,3},{3,2},{4,5},{5,4},{6,7},{7,6},{8,9},{9,8},{10,11... | collective-permute-start | bytes 1572872 | tf_op jit(solution)/shard_map/ppermute | solution.py:503
  1.9 0.7 pad_add_fusion.me
  2.6 6.5 %moments.1 = (f32[32,80,128]{2,1,0:T(8,128)}, f32[8,128]{1,0:T(8,128)}) custom-call(s32[32]{0:T(128)} %counts.5, s32[2]{0:T(128)} %pad_add_fusion.me, f32[32,8,512]{2,1,0:T(8,128)} %probes.1, f32[3,32,512]{2,1,0:T(8,128)} %bitcast.13, f32[3,32,64]{2,1,0:T(8,128)} %bitcast.16, f32[3,56,64]{2,1,0:T(8,128)} %bitcast.14), custom_call_target="tpu_custom_call" | custom-call | flops 8800000000 | bytes 1048576 | tf_op jit(solution)/shard_map/moments/pallas_call | solution.py:509
  9.0 0.7 broadcast_in_dim.2
  9.7 14.0 %all_to_all.5.roots = f32[32,8,128]{2,1,0:T(8,128)} all-to-all(f32[32,8,128]{2,1,0:T(8,128)S(1)} %broadcast_in_dim.2), channel_id=1, replica_groups=mesh['space'=32,'probe'=4] {'space'}, dimensions={0} | all-to-all | bytes 262144 | tf_op jit(solution)/shard_map/all_to_all | solution.py:519
  23.8 0.0 collective-permute-done.partner
  23.8 0.0 copy-start
  23.8 1.6 %pad_maximum_fusion = f32[32,112,128]{2,1,0:T(8,128)S(1)} fusion(f32[32,32,128]{2,1,0:T(8,128)S(1)} %bitcast.12, f32[32,80,128]{2,1,0:T(8,128)} %get-tuple-element.13.own.page), kind=kLoop, calls=%fused_computation | loop fusion | flops 458752 | bytes 3670016 | tf_op jit(solution)/shard_map/concatenate | solution.py:523
  25.4 0.0 copy-done
  25.4 2.0 %collective-permute-start.1 = (f32[32,112,128]{2,1,0:T(8,128)S(1)}, f32[32,112,128]{2,1,0:T(8,128)S(1)}, u32[]{:S(2)}, u32[]{:S(2)}) collective-permute-start(f32[32,112,128]{2,1,0:T(8,128)S(1)} %pad_maximum_fusion), channel_id=1, source_target_pairs={{0,4},{4,8},{8,12},{12,16},{16,20},{20,24},{24,28},{28,32},{32,36}... | collective-permute-start | bytes 5505032 | tf_op jit(solution)/shard_map/ppermute | solution.py:524
  27.5 5.6 %collective-permute-start.2 = (f32[32,112,128]{2,1,0:T(8,128)S(1)}, f32[32,112,128]{2,1,0:T(8,128)S(1)}, u32[]{:S(2)}, u32[]{:S(2)}) collective-permute-start(f32[32,112,128]{2,1,0:T(8,128)S(1)} %pad_maximum_fusion), channel_id=1, source_target_pairs={{4,0},{8,4},{12,8},{16,12},{20,16},{24,20},{28,24},{32,28},{36,32}... | collective-permute-start | bytes 5505032 | tf_op jit(solution)/shard_map/ppermute | solution.py:525
  33.1 0.0 copy-start.2
  33.1 27.8 %near_own.1.acc0 = f32[32,32,256]{2,1,0:T(8,128)} custom-call(s32[8,32]{1,0:T(8,128)} %bitcast.18, s32[32]{0:T(128)} %counts.5, s32[2]{0:T(128)} %pad_add_fusion.me, f32[32,80,128]{2,1,0:T(8,128)} %get-tuple-element.13.own.page, f32[32,8,512]{2,1,0:T(8,128)} %copy-done), custom_call_target="tpu_custom_call" | custom-call | flops 30799998976 | bytes 1048576 | tf_op jit(solution)/shard_map/near_own/pallas_call | solution.py:542
  60.9 0.0 collective-permute-done.2.high
  60.9 0.0 copy-start.4
  60.9 0.7 fusion
  61.6 0.0 collective-permute-done.1.low
  61.6 0.0 copy-start.3
  61.6 0.7 fusion.1
  62.3 0.0 copy-done.2
  62.3 0.6 pad_add_fusion.1.counts
  62.9 0.0 copy-done.4
  62.9 0.0 copy-done.3
  62.9 28.1 %near_halo.1 = (f32[16,8,512]{2,1,0:T(8,128)}, f32[16,8,512]{2,1,0:T(8,128)}) custom-call(s32[8,32]{1,0:T(8,128)} %bitcast.19, s32[96]{0:T(128)} %pad_add_fusion.1.counts, s32[2]{0:T(128)} %pad_add_fusion.me, f32[32,80,128]{2,1,0:T(8,128)} %get-tuple-element.13.own.page, f32[32,112,128]{2,1,0:T(8,128)} %copy-done.3, f32[32,112,128]{2,1,0:T(8,128)} %copy-done.4, ...), custom_call_target="tpu_custom_call" | custom-call | flops 32999999488 | bytes 1048576 | tf_op jit(solution)/shard_map/near_halo/pallas_call | solution.py:555
  90.9 0.1 collective-permute-start.3
  91.1 26.4 %far.2 = f32[32,8,512]{2,1,0:T(8,128)} custom-call(s32[32,32]{1,0:T(8,128)} %far.3, s32[16,56]{1,0:T(8,128)} %bitcast.17, s32[2]{0:T(128)} %pad_add_fusion.me, f32[32,80,128]{2,1,0:T(8,128)} %get-tuple-element.13.own.page, f32[32,112,128]{2,1,0:T(8,128)} %copy-done.3, f32[32,112,128]{2,1,0:T(8,128)} %copy-done.4, f32[3,56,64]{2,1,0:T(8,128)} %bitcast.15, ...), custom_call_target="tpu_custom_call" | custom-call | flops 32999999488 | bytes 1048576 | tf_op jit(solution)/shard_map/far/pallas_call | solution.py:568
  117.5 0.0 collective-permute-done.3.back
  117.5 0.0 copy-start.1
  117.5 0.7 copy-done.1
  118.2 2.8 %sum.1 = f32[32,8,512]{2,1,0:T(8,128)} custom-call(s32[32]{0:T(128)} %counts.5, s32[2]{0:T(128)} %pad_add_fusion.me, f32[32,8,512]{2,1,0:T(8,128)} %far.2, f32[16,8,512]{2,1,0:T(8,128)} %get-tuple-element.15.mine, f32[16,8,512]{2,1,0:T(8,128)} %copy-done.1), custom_call_target="tpu_custom_call" | custom-call | tf_op jit(solution)/shard_map/sum/pallas_call | solution.py:588
Async XLA Ops:
  0.0 23.8 %collective-permute-start = (f32[32,8,512]{2,1,0:T(8,128)}, f32[32,8,512]{2,1,0:T(8,128)S(1)}, u32[]{:S(2)}, u32[]{:S(2)}) collective-permute-start(f32[32,8,512]{2,1,0:T(8,128)} %probes.1), channel_id=1, source_target_pairs={{0,1},{1,0},{2,3},{3,2},{4,5},{5,4},{6,7},{7,6},{8,9},{9,8},{10,11... | collective-permute-start | bytes 1572872 | tf_op jit(solution)/shard_map/ppermute | solution.py:503
  23.8 1.6 %copy-start = (f32[32,8,512]{2,1,0:T(8,128)}, f32[32,8,512]{2,1,0:T(8,128)S(1)}, u32[]{:S(2)}) copy-start(f32[32,8,512]{2,1,0:T(8,128)S(1)} %collective-permute-done.partner) | copy-start | bytes 1572868
  25.4 36.2 %collective-permute-start.1 = (f32[32,112,128]{2,1,0:T(8,128)S(1)}, f32[32,112,128]{2,1,0:T(8,128)S(1)}, u32[]{:S(2)}, u32[]{:S(2)}) collective-permute-start(f32[32,112,128]{2,1,0:T(8,128)S(1)} %pad_maximum_fusion), channel_id=1, source_target_pairs={{0,4},{4,8},{8,12},{12,16},{16,20},{20,24},{24,28},{28,32},{32,36}... | collective-permute-start | bytes 5505032 | tf_op jit(solution)/shard_map/ppermute | solution.py:524
  27.5 33.5 %collective-permute-start.2 = (f32[32,112,128]{2,1,0:T(8,128)S(1)}, f32[32,112,128]{2,1,0:T(8,128)S(1)}, u32[]{:S(2)}, u32[]{:S(2)}) collective-permute-start(f32[32,112,128]{2,1,0:T(8,128)S(1)} %pad_maximum_fusion), channel_id=1, source_target_pairs={{4,0},{8,4},{12,8},{16,12},{20,16},{24,20},{28,24},{32,28},{36,32}... | collective-permute-start | bytes 5505032 | tf_op jit(solution)/shard_map/ppermute | solution.py:525
  33.1 29.2 %copy-start.2 = (s32[32]{0:T(128)S(1)}, s32[32]{0:T(128)}, u32[]{:S(2)}) copy-start(s32[32]{0:T(128)} %counts.5) | copy-start | bytes 388
  60.9 1.9 %copy-start.4 = (f32[32,112,128]{2,1,0:T(8,128)}, f32[32,112,128]{2,1,0:T(8,128)S(1)}, u32[]{:S(2)}) copy-start(f32[32,112,128]{2,1,0:T(8,128)S(1)} %collective-permute-done.2.high) | copy-start | bytes 5505028
  61.6 1.3 %copy-start.3 = (f32[32,112,128]{2,1,0:T(8,128)}, f32[32,112,128]{2,1,0:T(8,128)S(1)}, u32[]{:S(2)}) copy-start(f32[32,112,128]{2,1,0:T(8,128)S(1)} %collective-permute-done.1.low) | copy-start | bytes 5505028
  90.9 26.5 %collective-permute-start.3 = (f32[16,8,512]{2,1,0:T(8,128)}, f32[16,8,512]{2,1,0:T(8,128)S(1)}, u32[]{:S(2)}, u32[]{:S(2)}) collective-permute-start(f32[16,8,512]{2,1,0:T(8,128)} %get-tuple-element.16), channel_id=1, source_target_pairs={{0,1},{1,0},{2,3},{3,2},{4,5},{5,4},{6,7},{7,6},{8,9},{9,8},{10,11... | collective-permute-start | bytes 786440 | tf_op jit(solution)/shard_map/ppermute | solution.py:565
  117.5 0.7 copy-start.1
where the time goes:
time: 121 us
  Pallas kernels  91.5 us (76%)
  blocking collectives  14 us (12%)
  starting transfers between devices  9.73 us (8%)
  other arithmetic  4.19 us (3%)
  local copies, waits for them, and re-layouts  1.42 us (1%)
    pallas_call x1, Pallas kernels, local(): pl.pallas_call(functools.partial(halo_kernel, leaves=leaves, targets=targ...  28.1 us
    pallas_call x1, Pallas kernels, local(): pl.pallas_call(functools.partial(own_kernel, leaves=leaves, targets=targe...  27.8 us
    pallas_call x1, Pallas kernels, local(): pl.pallas_call(functools.partial(far_kernel, leaves=leaves, factor=factor...  26.4 us
    all_to_all x1, blocking collectives, local(): lax.all_to_all(jnp.broadcast_to(dev[None], (nodes, 8, 128)), 'space', spl...  14 us
    pallas_call x1, Pallas kernels, local(): pl.pallas_call(functools.partial(moments_kernel, leaves=leaves, factor=fa...  6.46 us
    ppermute x1, starting transfers between devices, local(): high = lax.ppermute(both, 'space', backward)  5.64 us
    pallas_call x1, Pallas kernels, local(): pl.pallas_call(functools.partial(sum_kernel, leaves=leaves), out_shape=sh...  2.79 us
  transfers between devices with their start and end apart: 4, of which 0 were waited for; matrix products, arithmetic and copies ran while one was open for 2% of the time, Pallas kernels for 50%

commit v1 on v0

--- a/solution.py
+++ b/solution.py
@@ -15,7 +15,7 @@
 SLOPE = 0.5 / (LOG2E * LOG2E)
 TINY = 1e-30
 FEATURES = 48
-UNITS = 8
+UNITS = 12
 CN = (((0,), (0,)), ((), ()))
 NT = (((1,), (1,)), ((), ()))
 NN = (((1,), (0,)), ((), ()))
@@ -363,12 +363,12 @@
 
 def upper_levels(coarse, me, box8, roots, c, fbs, fbt, pm, qm):
     def prep(t, carry):
-        for s in range(8):
-            b = 8 * t + s
+        for s in range(14):
+            b = 14 * t + s
             fbs[b], fbt[b] = features(twice(rows_of(box8, b, 0.0)), c, True, True)
         return carry
 
-    lax.fori_loop(0, 7, prep, 0)
+    lax.fori_loop(0, 4, prep, 0)
     half = left_half((FEATURES, 128))
     half8 = left_half((8, 128))
 
@@ -415,28 +415,28 @@
     c = center_of(own)
 
     def prep_far(t, carry):
-        for s in range(4):
-            i = t * 4 + s
+        for s in range(8):
+            i = t * 8 + s
             for k, (page, at) in enumerate(((low, 0), (own, 64), (high, 0))):
                 (fps[k * leaves + i],) = features(page[i, at + 8 : at + 16], c, True, False)
                 mps[k * leaves + i] = page[i, at : at + 8]
             (fpt[i],) = features(own[i, 72:80], c, False, True)
         return carry
 
-    lax.fori_loop(0, leaves // 4, prep_far, 0)
+    lax.fori_loop(0, leaves // 8, prep_far, 0)
     dev = me[0]
     base = (dev - 1) * leaves
 
     def gather(t, carry):
-        for s in range(2):
-            k = t * 2 + s
+        for s in range(4):
+            k = t * 4 + s
             local[k] = far_pair(
                 [lambda e: far[2 * k, e] - base, lambda e: far[2 * k + 1, e] - base],
                 lambda b: fps[b], lambda b: mps[b], shared(fpt[2 * k], fpt[2 * k + 1]),
             )
         return carry
 
-    lax.fori_loop(0, leaves // 4, gather, 0)
+    lax.fori_loop(0, leaves // 8, gather, 0)
     local_dev = upper_levels(coarse, dev, box8, roots, c, fbs, fbt, pm, qm)
     own_source = fbs[dev].astype(BF16)[:, :64]
     half = left_half((FEATURES, 128))
@@ -452,16 +452,16 @@
     lax.fori_loop(0, leaves // 16, down, 0)
 
     def finish(t, carry):
-        for s in range(8):
-            i = t * 8 + s
+        for s in range(16):
+            i = t * 16 + s
             source = fps[leaves + i].astype(BF16)[:, :64]
             (points,) = features(lanes_of(own, i, 8), c, False, True)
             basis = value_of(dot(source, points.astype(BF16), CN))
-            part = local[t * 4 + s // 2][:, (s % 2) * 64 : (s % 2) * 64 + 64]
+            part = local[t * 8 + s // 2][:, (s % 2) * 64 : (s % 2) * 64 + 64]
             out[i] = exact_dot(part, basis, NN) * factor
         return carry
 
-    lax.fori_loop(0, leaves // 8, finish, 0)
+    lax.fori_loop(0, leaves // 16, finish, 0)
 
 
 def sum_kernel(counts, me, far, mine, back, out, order, *, leaves):
@@ -532,7 +532,7 @@
                 vm((blocks, 32, 128), BF16),
                 vm((targets * 2, FEATURES, 256), BF16),
                 pltpu.SMEM((48,), jnp.int32),
-                pltpu.SMEM((targets * 32 + 64,), jnp.int32),
+                pltpu.SMEM((targets * 32 + 96,), jnp.int32),
                 pltpu.SMEM((leaves,), jnp.int32),
             ]
             + [vm((256, 256), F32)] * UNITS

time: 121 us -> 118 us (0.975)
  the two profiles are of different devices: /device:TPU:8 before, /device:TPU:48 now
where the time goes in v1:
time: 118 us; the launch traced here: 116 us
  Pallas kernels  86.7 us (73%)
  blocking collectives  13.1 us (11%)
  starting transfers between devices  11 us (9%)
  other arithmetic  4.19 us (4%)
  local copies, waits for them, and re-layouts  1.42 us (1%)
    pallas_call x1, Pallas kernels, local(): pl.pallas_call(functools.partial(halo_kernel, leaves=leaves, targets=targ...  30.1 us
    pallas_call x1, Pallas kernels, local(): pl.pallas_call(functools.partial(far_kernel, leaves=leaves, factor=factor...  24.4 us
    pallas_call x1, Pallas kernels, local(): pl.pallas_call(functools.partial(own_kernel, leaves=leaves, targets=targe...  22.9 us
    all_to_all x1, blocking collectives, local(): lax.all_to_all(jnp.broadcast_to(dev[None], (nodes, 8, 128)), 'space', spl...  13.1 us
    pallas_call x1, Pallas kernels, local(): pl.pallas_call(functools.partial(moments_kernel, leaves=leaves, factor=fa...  6.46 us
    ppermute x1, starting transfers between devices, local(): high = lax.ppermute(both, 'space', backward)  5.59 us
    ppermute x1, starting transfers between devices, local(): back = lax.ppermute(theirs, 'probe', pairs)  3.2 us
    pallas_call x1, Pallas kernels, local(): pl.pallas_call(functools.partial(sum_kernel, leaves=leaves), out_shape=sh...  2.79 us
  transfers between devices with their start and end apart: 4, of which 0 were waited for; matrix products, arithmetic and copies ran while one was open for 2% of the time, Pallas kernels for 46%

profile of v1, /device:TPU:48, one launch (start us, length us, event | category | flops | bytes accessed | tf_op | source)
XLA Modules:
  0.0 116.4 jit_solution(14844263739796301539)
XLA Ops:
  0.0 0.1 collective-permute-start
  0.1 0.7 pad_add_fusion.me
  0.8 6.5 %moments.1 = (f32[32,80,128]{2,1,0:T(8,128)}, f32[8,128]{1,0:T(8,128)}) custom-call(s32[32]{0:T(128)} %counts.5, s32[2]{0:T(128)} %pad_add_fusion.me, f32[32,8,512]{2,1,0:T(8,128)} %probes.1, f32[3,32,512]{2,1,0:T(8,128)} %bitcast.13, f32[3,32,64]{2,1,0:T(8,128)} %bitcast.16, f32[3,56,64]{2,1,0:T(8,128)} %bitcast.14), custom_call_target="tpu_custom_call" | custom-call | flops 8800000000 | bytes 1048576 | tf_op jit(solution)/shard_map/moments/pallas_call | solution.py:509
  7.2 0.7 broadcast_in_dim.2
  7.9 13.1 %all_to_all.5.roots = f32[32,8,128]{2,1,0:T(8,128)} all-to-all(f32[32,8,128]{2,1,0:T(8,128)S(1)} %broadcast_in_dim.2), channel_id=1, replica_groups=mesh['space'=32,'probe'=4] {'space'}, dimensions={0} | all-to-all | bytes 262144 | tf_op jit(solution)/shard_map/all_to_all | solution.py:519
  21.0 0.0 collective-permute-done.partner
  21.0 0.0 copy-start
  21.0 1.6 %pad_maximum_fusion = f32[32,112,128]{2,1,0:T(8,128)S(1)} fusion(f32[32,32,128]{2,1,0:T(8,128)S(1)} %bitcast.12, f32[32,80,128]{2,1,0:T(8,128)} %get-tuple-element.13.own.page), kind=kLoop, calls=%fused_computation | loop fusion | flops 458752 | bytes 3670016 | tf_op jit(solution)/shard_map/concatenate | solution.py:523
  22.6 0.0 copy-done
  22.6 2.1 %collective-permute-start.1 = (f32[32,112,128]{2,1,0:T(8,128)S(1)}, f32[32,112,128]{2,1,0:T(8,128)S(1)}, u32[]{:S(2)}, u32[]{:S(2)}) collective-permute-start(f32[32,112,128]{2,1,0:T(8,128)S(1)} %pad_maximum_fusion), channel_id=1, source_target_pairs={{0,4},{4,8},{8,12},{12,16},{16,20},{20,24},{24,28},{28,32},{32,36}... | collective-permute-start | bytes 5505032 | tf_op jit(solution)/shard_map/ppermute | solution.py:524
  24.7 5.6 %collective-permute-start.2 = (f32[32,112,128]{2,1,0:T(8,128)S(1)}, f32[32,112,128]{2,1,0:T(8,128)S(1)}, u32[]{:S(2)}, u32[]{:S(2)}) collective-permute-start(f32[32,112,128]{2,1,0:T(8,128)S(1)} %pad_maximum_fusion), channel_id=1, source_target_pairs={{4,0},{8,4},{12,8},{16,12},{20,16},{24,20},{28,24},{32,28},{36,32}... | collective-permute-start | bytes 5505032 | tf_op jit(solution)/shard_map/ppermute | solution.py:525
  30.3 0.0 copy-start.2
  30.3 22.9 %near_own.1.acc0 = f32[32,32,256]{2,1,0:T(8,128)} custom-call(s32[8,32]{1,0:T(8,128)} %bitcast.18, s32[32]{0:T(128)} %counts.5, s32[2]{0:T(128)} %pad_add_fusion.me, f32[32,80,128]{2,1,0:T(8,128)} %get-tuple-element.13.own.page, f32[32,8,512]{2,1,0:T(8,128)} %copy-done), custom_call_target="tpu_custom_call" | custom-call | flops 30799998976 | bytes 1048576 | tf_op jit(solution)/shard_map/near_own/pallas_call | solution.py:542
  53.2 0.0 collective-permute-done.2.high
  53.2 0.0 copy-start.4
  53.2 0.7 fusion
  53.9 0.0 collective-permute-done.1.low
  53.9 0.0 copy-start.3
  53.9 0.7 fusion.1
  54.6 0.0 copy-done.2
  54.6 0.6 pad_add_fusion.1.counts
  55.1 0.0 copy-done.4
  55.1 0.0 copy-done.3
  55.2 30.1 %near_halo.1 = (f32[16,8,512]{2,1,0:T(8,128)}, f32[16,8,512]{2,1,0:T(8,128)}) custom-call(s32[8,32]{1,0:T(8,128)} %bitcast.19, s32[96]{0:T(128)} %pad_add_fusion.1.counts, s32[2]{0:T(128)} %pad_add_fusion.me, f32[32,80,128]{2,1,0:T(8,128)} %get-tuple-element.13.own.page, f32[32,112,128]{2,1,0:T(8,128)} %copy-done.3, f32[32,112,128]{2,1,0:T(8,128)} %copy-done.4, ...), custom_call_target="tpu_custom_call" | custom-call | flops 32999999488 | bytes 1048576 | tf_op jit(solution)/shard_map/near_halo/pallas_call | solution.py:555
  85.3 3.2 %collective-permute-start.3 = (f32[16,8,512]{2,1,0:T(8,128)}, f32[16,8,512]{2,1,0:T(8,128)S(1)}, u32[]{:S(2)}, u32[]{:S(2)}) collective-permute-start(f32[16,8,512]{2,1,0:T(8,128)} %get-tuple-element.16), channel_id=1, source_target_pairs={{0,1},{1,0},{2,3},{3,2},{4,5},{5,4},{6,7},{7,6},{8,9},{9,8},{10,11... | collective-permute-start | bytes 786440 | tf_op jit(solution)/shard_map/ppermute | solution.py:565
  88.5 24.4 %far.2 = f32[32,8,512]{2,1,0:T(8,128)} custom-call(s32[32,32]{1,0:T(8,128)} %far.3, s32[16,56]{1,0:T(8,128)} %bitcast.17, s32[2]{0:T(128)} %pad_add_fusion.me, f32[32,80,128]{2,1,0:T(8,128)} %get-tuple-element.13.own.page, f32[32,112,128]{2,1,0:T(8,128)} %copy-done.3, f32[32,112,128]{2,1,0:T(8,128)} %copy-done.4, f32[3,56,64]{2,1,0:T(8,128)} %bitcast.15, ...), custom_call_target="tpu_custom_call" | custom-call | flops 32999999488 | bytes 1048576 | tf_op jit(solution)/shard_map/far/pallas_call | solution.py:568
  112.9 0.0 collective-permute-done.3.back
  112.9 0.0 copy-start.1
  112.9 0.7 copy-done.1
  113.6 2.8 %sum.1 = f32[32,8,512]{2,1,0:T(8,128)} custom-call(s32[32]{0:T(128)} %counts.5, s32[2]{0:T(128)} %pad_add_fusion.me, f32[32,8,512]{2,1,0:T(8,128)} %far.2, f32[16,8,512]{2,1,0:T(8,128)} %get-tuple-element.15.mine, f32[16,8,512]{2,1,0:T(8,128)} %copy-done.1), custom_call_target="tpu_custom_call" | custom-call | tf_op jit(solution)/shard_map/sum/pallas_call | solution.py:588
Async XLA Ops:
  0.0 21.0 %collective-permute-start = (f32[32,8,512]{2,1,0:T(8,128)}, f32[32,8,512]{2,1,0:T(8,128)S(1)}, u32[]{:S(2)}, u32[]{:S(2)}) collective-permute-start(f32[32,8,512]{2,1,0:T(8,128)} %probes.1), channel_id=1, source_target_pairs={{0,1},{1,0},{2,3},{3,2},{4,5},{5,4},{6,7},{7,6},{8,9},{9,8},{10,11... | collective-permute-start | bytes 1572872 | tf_op jit(solution)/shard_map/ppermute | solution.py:503
  21.0 1.6 %copy-start = (f32[32,8,512]{2,1,0:T(8,128)}, f32[32,8,512]{2,1,0:T(8,128)S(1)}, u32[]{:S(2)}) copy-start(f32[32,8,512]{2,1,0:T(8,128)S(1)} %collective-permute-done.partner) | copy-start | bytes 1572868
  22.6 31.2 %collective-permute-start.1 = (f32[32,112,128]{2,1,0:T(8,128)S(1)}, f32[32,112,128]{2,1,0:T(8,128)S(1)}, u32[]{:S(2)}, u32[]{:S(2)}) collective-permute-start(f32[32,112,128]{2,1,0:T(8,128)S(1)} %pad_maximum_fusion), channel_id=1, source_target_pairs={{0,4},{4,8},{8,12},{12,16},{16,20},{20,24},{24,28},{28,32},{32,36}... | collective-permute-start | bytes 5505032 | tf_op jit(solution)/shard_map/ppermute | solution.py:524
  24.7 28.5 %collective-permute-start.2 = (f32[32,112,128]{2,1,0:T(8,128)S(1)}, f32[32,112,128]{2,1,0:T(8,128)S(1)}, u32[]{:S(2)}, u32[]{:S(2)}) collective-permute-start(f32[32,112,128]{2,1,0:T(8,128)S(1)} %pad_maximum_fusion), channel_id=1, source_target_pairs={{4,0},{8,4},{12,8},{16,12},{20,16},{24,20},{28,24},{32,28},{36,32}... | collective-permute-start | bytes 5505032 | tf_op jit(solution)/shard_map/ppermute | solution.py:525
  30.3 24.2 %copy-start.2 = (s32[32]{0:T(128)S(1)}, s32[32]{0:T(128)}, u32[]{:S(2)}) copy-start(s32[32]{0:T(128)} %counts.5) | copy-start | bytes 388
  53.2 1.9 %copy-start.4 = (f32[32,112,128]{2,1,0:T(8,128)}, f32[32,112,128]{2,1,0:T(8,128)S(1)}, u32[]{:S(2)}) copy-start(f32[32,112,128]{2,1,0:T(8,128)S(1)} %collective-permute-done.2.high) | copy-start | bytes 5505028
  53.9 1.3 %copy-start.3 = (f32[32,112,128]{2,1,0:T(8,128)}, f32[32,112,128]{2,1,0:T(8,128)S(1)}, u32[]{:S(2)}) copy-start(f32[32,112,128]{2,1,0:T(8,128)S(1)} %collective-permute-done.1.low) | copy-start | bytes 5505028
  85.3 27.6 %collective-permute-start.3 = (f32[16,8,512]{2,1,0:T(8,128)}, f32[16,8,512]{2,1,0:T(8,128)S(1)}, u32[]{:S(2)}, u32[]{:S(2)}) collective-permute-start(f32[16,8,512]{2,1,0:T(8,128)} %get-tuple-element.16), channel_id=1, source_target_pairs={{0,1},{1,0},{2,3},{3,2},{4,5},{5,4},{6,7},{7,6},{8,9},{9,8},{10,11... | collective-permute-start | bytes 786440 | tf_op jit(solution)/shard_map/ppermute | solution.py:565
  112.9 0.7 copy-start.1
